TPU v7x, 32 devices: a whole 2x2x4 slice. The times are simulated.
32 devices in a mesh: group: 1, expert: 16 (over z, y, x), dp: 2 (over core).
Axes of the slice: x: 2, y: 2, z: 4, core: 2. Of those that a mesh axis runs over, the one named last changes fastest.
Arguments:
- tokens: bfloat16 [2048, 4096], P(('group', 'expert', 'dp')), may hold values from -6 to 6
- queries: bfloat16 [2048, 4096], P(('group', 'expert', 'dp')), may hold values from -6 to 6
- keys_local: bfloat16 [2048, 256], P(('group', 'expert', 'dp')), may hold values from -6 to 6
- values_local: bfloat16 [2048, 256], P(('group', 'expert', 'dp')), may hold values from -6 to 6
- prompt_keys: bfloat16 [1024, 256], P('group'), may hold values from -6 to 6
- prompt_values: bfloat16 [1024, 256], P('group'), may hold values from -6 to 6
- norm_gain: float32 [4096], replicated, may hold values from 0.25 to 1.75
- expert_ids: int32 [2048, 8], P(('group', 'expert', 'dp')), may hold values from 0 to 15, all different within a row; in each aligned block of 64 rows (0 to 63, 64 to 127, ...) at most 42 rows name the same one
- route_weight: float32 [2048, 8], P(('group', 'expert', 'dp')), may hold values from 0.05 to 1
- stored_gate: bfloat16 [16, 4096, 768], P('expert', None, 'dp'), may hold values from -0.09375 to 0.09375
- stored_up: bfloat16 [16, 4096, 768], P('expert', None, 'dp'), may hold values from -0.09375 to 0.09375
- stored_down: bfloat16 [16, 768, 4096], P('expert', 'dp'), may hold values from -0.21875 to 0.21875
- holder: int32 [16], replicated, may hold values from 0 to 15, as said below
Outputs:
- layer_out: bfloat16 [2048, 4096], P(('group', 'expert', 'dp'))
Inputs may be any that keep to these rules, and one draw needn't show every extreme that they name: `expert_ids`: each row names 8 different experts. In the 64 rows of one device no expert is named more than 42 times, and in every draw some expert is named exactly 42 times in some device's rows. holder[s] is s or the slot 8 away (s + 16 / 2 modulo 16), holder[holder[s]] = s, and holder[0] = 8.
All inputs are finite; a program needn't handle non-finite values.
Results may differ from a plain program's by a relative error of at most 0.0055.
Values may be sent and summed in bfloat16 or wider, within the bound.
No kernel may reach another device: no remote copies, remote signals or barrier semaphores. Data moves between devices by JAX's collectives and lax.ppermute only.
A program may use at most 192 MiB of HBM per device.

v0:
```python
import jax
import jax.numpy as jnp
from jax import lax
from jax.sharding import PartitionSpec as P

HEADS = 32
KVH = 2
HD = 128
TOPK = 8
EXP_DEV = 1
PREFIX = 1024


def attend_rows(queries, keys_local, values_local, prompt_keys, prompt_values):
    count_rows = queries.shape[0]
    grouping = HEADS // KVH
    query_all = queries.reshape(count_rows, KVH, grouping, HD)
    key_all = jnp.concatenate([prompt_keys, keys_local], 0).reshape(-1, KVH, HD)
    value_all = jnp.concatenate([prompt_values, values_local], 0).reshape(-1, KVH, HD)
    scores = jnp.einsum(
        "tkgd,skd->kgts", query_all, key_all, preferred_element_type=jnp.float32
    ) * HD ** (-0.5)
    column = jnp.arange(key_all.shape[0], dtype=jnp.int32)
    row_index = jnp.arange(count_rows, dtype=jnp.int32)
    allowed = (column[None, :] < PREFIX) | (column[None, :] - PREFIX <= row_index[:, None])
    scores = jnp.where(allowed[None, None], scores, -jnp.inf)
    highest = jnp.max(scores, axis=-1, keepdims=True)
    expons = jnp.exp(scores - highest)
    weights = (expons / jnp.sum(expons, axis=-1, keepdims=True)).astype(jnp.bfloat16)
    context = jnp.einsum("kgts,skd->tkgd", weights, value_all, preferred_element_type=jnp.float32)
    return context.reshape(count_rows, HEADS * HD)


def expert_rows(picked, gate_w, up_w, down_w):
    gate_val = jnp.dot(picked, gate_w, preferred_element_type=jnp.float32)
    up_val = jnp.dot(picked, up_w, preferred_element_type=jnp.float32)
    hidden = (jax.nn.silu(gate_val) * up_val).astype(jnp.bfloat16)
    return jnp.dot(hidden, down_w, preferred_element_type=jnp.float32).astype(jnp.bfloat16)


def local(
    tokens,
    queries,
    keys_local,
    values_local,
    prompt_keys,
    prompt_values,
    norm_gain,
    expert_ids,
    route_weight,
    stored_gate,
    stored_up,
    stored_down,
    holder,
):
    owners = lax.axis_size("expert")
    tok_count = tokens.shape[0]
    model_width = tokens.shape[1]
    capacity = min(tok_count, max(2, tok_count * TOPK * 4 // (3 * owners * EXP_DEV)))
    gate_w = stored_gate[0]
    up_w = stored_up[0]
    down_w = stored_down[0]
    context = attend_rows(queries, keys_local, values_local, prompt_keys, prompt_values)
    widened = tokens.astype(jnp.float32)
    normed = (
        widened * lax.rsqrt(jnp.mean(widened * widened, axis=-1, keepdims=True) + 1e-06) * norm_gain
    ).astype(jnp.bfloat16)
    shares = route_weight / jnp.sum(route_weight, axis=-1, keepdims=True)
    flat_ids = expert_ids.reshape(-1)
    onehot = (flat_ids[:, None] == jnp.arange(owners, dtype=jnp.int32)[None, :]).astype(jnp.int32)
    earlier = jnp.cumsum(onehot, axis=0) - onehot
    slot_of = jnp.sum(earlier * onehot, axis=1)
    places = (holder[flat_ids] * capacity + slot_of).reshape(tok_count, TOPK)
    chooser = (
        (jnp.arange(owners * capacity, dtype=jnp.int32)[:, None, None] == places[None])
        .any(axis=2)
        .astype(jnp.bfloat16)
    )
    send_rows = (
        jnp.dot(chooser, normed, preferred_element_type=jnp.float32)
        .astype(jnp.bfloat16)
        .reshape(owners, capacity, model_width)
    )
    both_rows = lax.all_gather(
        lax.all_to_all(send_rows, "expert", split_axis=0, concat_axis=0, tiled=True)[None],
        "dp",
        axis=0,
        tiled=True,
    )
    partial_out = expert_rows(both_rows.reshape(-1, model_width), gate_w, up_w, down_w)
    partial_out = partial_out.astype(jnp.float32).reshape(both_rows.shape)
    own_sum = lax.psum_scatter(
        partial_out.astype(jnp.bfloat16), "dp", scatter_dimension=0, tiled=True
    ).astype(jnp.float32)[0]
    results = lax.all_to_all(
        own_sum.astype(jnp.bfloat16), "expert", split_axis=0, concat_axis=0, tiled=True
    )
    gathered = results.reshape(owners * capacity, model_width)[places]
    mixture = jnp.einsum("tk,tkd->td", shares, gathered.astype(jnp.float32))
    return (widened + context + mixture).astype(jnp.bfloat16)


def solution(mesh):
    return jax.shard_map(
        local,
        mesh=mesh,
        in_specs=(
            P(("group", "expert", "dp"), None),
            P(("group", "expert", "dp"), None),
            P(("group", "expert", "dp"), None),
            P(("group", "expert", "dp"), None),
            P("group", None),
            P("group", None),
            P(),
            P(("group", "expert", "dp"), None),
            P(("group", "expert", "dp"), None),
            P("expert", None, "dp"),
            P("expert", None, "dp"),
            P("expert", "dp", None),
            P(),
        ),
        out_specs=P(("group", "expert", "dp"), None),
        check_vma=False,
    )
```

profile of v0, /device:TPU:14, one launch (start us, length us, event | category | flops | bytes accessed | tf_op | source)
XLA Modules:
  0.0 474.5 jit_solution(1100816948195221598)
XLA Ops:
  6.5 0.9 copy.43
  7.7 2.0 fusion.56
  9.7 4.4 compare_select_fusion.2
  14.2 1.2 reduce-window.6
  15.3 0.2 slice_reduce_fusion
  15.7 5.6 %fusion.48 = s32[512]{0:T(512)S(1)} fusion(s32[512]{0:T(512)S(1)} %fusion.46, pred[512]{0:T(512)(128)(4,1)S(1)} %get-tuple-element.13, pred[512]{0:T(512)(128)(4,1)S(1)} %get-tuple-element.12, pred[512]{0:T(512)(128)(4,1)S(1)} %get-tuple-element.11, pred[512]{0:T(512)(128)(4,1)S(1)} %get-tuple-element.10, pred[512]{0:T(512)(128)(4,1)S(1)} %get-tuple-element.9, ...), kind=kLoop, calls=%fused_computation.76 | loop fusion | flops 5632 | bytes 10788 | tf_op jit(solution)/shard_map/add | solution.py:73
  21.4 0.5 fusion.20
  21.9 1.2 fusion.26
  23.2 5.2 %convolution_convert_fusion.1 = bf16[672,4096]{1,0:T(8,128)(2,1)} fusion(pred[672,64]{0,1:T(8,128)(4,1)S(1)} %fusion.20, bf16[64,4096]{1,0:T(8,128)(2,1)} %param.13, f32[4096]{0:T(1024)} %param.19, f32[64]{0:T(128)S(1)} %add_rsqrt_fusion), kind=kOutput, calls=%fused_computation.7 | convolution fusion | flops 356122624 | bytes 6088960 | tf_op jit(solution)/shard_map/dot_general | solution.py:80
  28.3 6.2 %reshape.183 = bf16[16,42,4096]{2,1,0:T(8,128)(2,1)} reshape(bf16[672,4096]{1,0:T(8,128)(2,1)} %convolution_convert_fusion.1) | data formatting | bytes 11010048 | tf_op jit(solution)/shard_map/reshape | solution.py:82
  34.5 143.7 %all_to_all.10 = bf16[16,42,4096]{2,1,0:T(8,128)(2,1)S(1)} all-to-all(bf16[16,42,4096]{2,1,0:T(8,128)(2,1)} %reshape.183), channel_id=1, replica_groups=mesh['group'=1,'expert'=16,'dp'=2] {'expert'}, dimensions={0} | all-to-all | bytes 11010048 | tf_op jit(solution)/shard_map/all_to_all | solution.py:85
  178.3 5.4 %copy.47 = bf16[16,42,4096]{2,0,1:T(8,128)(2,1)} copy(bf16[16,42,4096]{2,1,0:T(8,128)(2,1)S(1)} %all_to_all.10) | data formatting | bytes 11010048 | tf_op jit(solution)/shard_map/all_to_all | solution.py:85
  183.7 0.2 reduce-scatter.2.cloned.1.call-start
  183.9 23.3 %all-gather.3.cloned.1.call-done = bf16[32,42,4096]{2,0,1:T(8,128)(2,1)} async-done(((bf16[16,42,4096]{2,0,1:T(8,128)(2,1)}), bf16[32,42,4096]{2,0,1:T(8,128)(2,1)}) %all-gather.3.cloned.1.call-update) | async-done | bytes 11010064 | tf_op jit(solution)/shard_map/all_gather | solution.py:84
  207.3 14.0 %copy.48 = bf16[32,42,4096]{2,1,0:T(8,128)(2,1)} copy(bf16[32,42,4096]{2,0,1:T(8,128)(2,1)} %all-gather.3.cloned.1.call-done) | data formatting | bytes 22020096 | tf_op jit(solution)/shard_map/all_gather | solution.py:84
  221.3 11.9 %reshape.184 = bf16[1344,4096]{1,0:T(8,128)(2,1)} reshape(bf16[32,42,4096]{2,1,0:T(8,128)(2,1)} %copy.48) | data formatting | bytes 22020096 | tf_op jit(solution)/shard_map/reshape | solution.py:90
  233.2 10.5 %fusion.10 = f32[1344,384]{1,0:T(8,128)} fusion(bf16[1344,4096]{1,0:T(8,128)(2,1)} %reshape.184, bf16[1,4096,384]{2,1,0:T(8,128)(2,1)} %param.22), kind=kOutput, calls=%fused_computation.17 | convolution fusion | flops 4227858432 | bytes 16220160 | tf_op jit(solution)/shard_map/dot_general | solution.py:35
  243.7 17.9 %convolution_convert_fusion = bf16[1344,4096]{1,0:T(8,128)(2,1)} fusion(bf16[1,384,4096]{2,1,0:T(8,128)(2,1)S(1)} %copy-done, bf16[1344,4096]{1,0:T(8,128)(2,1)} %reshape.184, bf16[1,4096,384]{2,1,0:T(8,128)(2,1)} %param.23, f32[1344,384]{1,0:T(8,128)} %fusion.10), kind=kOutput, calls=%fused_computation.2 | convolution fusion | flops 8464318464 | bytes 30375936 | tf_op jit(solution)/shard_map/dot_general | solution.py:38
  261.6 11.7 %convert_element_type.48 = bf16[2,16,42,4096]{3,2,1,0:T(8,128)(2,1)} reshape(bf16[1344,4096]{1,0:T(8,128)(2,1)} %convolution_convert_fusion) | data formatting | bytes 22020096 | tf_op jit(solution)/shard_map/convert_element_type | solution.py:93
  273.4 23.3 %reduce-scatter.2.cloned.1.call-done = bf16[1,16,42,4096]{3,2,1,0:T(8,128)(2,1)} async-done(((bf16[2,16,42,4096]{3,2,1,0:T(8,128)(2,1)}), bf16[1,16,42,4096]{3,2,1,0:T(8,128)(2,1)}) %reduce-scatter.2.cloned.1.call-update) | async-done | bytes 5505040 | tf_op jit(solution)/shard_map/reduce_scatter | solution.py:92
  296.7 7.1 %all-to-all-start.1 = ((bf16[16,42,4096]{2,1,0:T(8,128)(2,1)}), bf16[16,42,4096]{2,1,0:T(8,128)(2,1)}, u32[]{:S(2)}, u32[]{:S(2)}) async-start(bf16[16,42,4096]{2,1,0:T(8,128)(2,1)} %bitcast.96), calls=%async_computation.2 | async-start | bytes 12582912 | tf_op jit(solution)/shard_map/all_to_all | solution.py:95
  304.2 0.3 copy.38
  304.5 0.9 copy.58
  305.4 0.3 copy.37
  305.8 4.3 fusion.57
  310.1 5.9 %fusion.21 = f32[64,2,16,128]{3,0,2,1:T(8,128)S(1)} fusion(bf16[1088,2,128,1]{0,2,3,1:T(8,128)(2,1)S(1)} %bitcast.100, f32[2,16,64]{2,1,0:T(8,128)S(1)} %fusion.57, pred[64,1088]{1,0:T(8,128)(4,1)S(1)} %fusion.39, bf16[1088,2,128,1]{0,2,3,1:T(8,128)(2,1)S(1)} %bitcast.99, bf16[64,2,16,128]{3,2,1,0:T(8,128)(2,1)} %bitcast.103), kind=kOutput, calls=%fused_computation.28 | convolution fusion | flops 1151994880 | bytes 2764800 | tf_op jit(solution)/shard_map/kgts,skd->tkgd/dot_general | solution.py:30
  316.0 1.6 copy.42
  317.6 126.1 %all-to-all-done.1 = bf16[16,42,4096]{2,1,0:T(8,128)(2,1)} async-done(((bf16[16,42,4096]{2,1,0:T(8,128)(2,1)}), bf16[16,42,4096]{2,1,0:T(8,128)(2,1)}, u32[]{:S(2)}, u32[]{:S(2)}) %all-to-all-start.1) | async-done | bytes 5505056 | tf_op jit(solution)/shard_map/all_to_all | solution.py:95
  443.7 6.2 %reshape.185 = bf16[672,4096]{1,0:T(8,128)(2,1)} reshape(bf16[16,42,4096]{2,1,0:T(8,128)(2,1)} %all-to-all-done.1) | data formatting | bytes 11010048 | tf_op jit(solution)/shard_map/reshape | solution.py:98
  449.9 12.2 %gather_fusion = bf16[512,4096]{1,0:T(8,128)(2,1)} fusion(bf16[672,4096]{1,0:T(8,128)(2,1)} %reshape.185, s32[1024]{0:T(1024)S(1)} %pad_clamp_fusion), kind=kCustom, calls=%fused_computation | custom fusion | bytes 8390656 | tf_op jit(solution)/shard_map/gather | solution.py:98
  462.1 3.5 fusion.6
  465.7 1.9 fusion.25
  (45 shorter events, 1.1 us)
Async XLA Ops:
  6.5 237.2 %copy-start = (bf16[1,384,4096]{2,1,0:T(8,128)(2,1)S(1)}, bf16[1,384,4096]{2,1,0:T(8,128)(2,1)}, u32[]{:S(2)}) copy-start(bf16[1,384,4096]{2,1,0:T(8,128)(2,1)} %param.24) | copy-start | bytes 9437188
  6.5 200.7 %all-gather.3.cloned.1.call-start = ((), (), s32[]{:S(2)}) async-start(), calls=%async_computation.4 | async-start | bytes 16515072 | tf_op jit(solution)/shard_map/all_gather | solution.py:84
  183.7 112.9 %reduce-scatter.2.cloned.1.call-start = ((), (), s32[]{:S(2)}) async-start(), calls=%async_computation.3 | async-start | bytes 18874368 | tf_op jit(solution)/shard_map/reduce_scatter | solution.py:92
  296.6 7.3 %copy-start.9 = (f32[64,8]{0,1:T(8,128)S(1)}, f32[64,8]{0,1:T(8,128)}, u32[]{:S(2)}) copy-start(f32[64,8]{0,1:T(8,128)} %param.21) | copy-start | bytes 6148
  296.6 7.5 %copy-start.4 = (bf16[1024,256]{1,0:T(8,128)(2,1)S(1)}, bf16[1024,256]{1,0:T(8,128)(2,1)}, u32[]{:S(2)}) copy-start(bf16[1024,256]{1,0:T(8,128)(2,1)} %param.17) | copy-start | bytes 1572868
  296.6 7.5 %copy-start.7 = (bf16[64,256]{1,0:T(8,128)(2,1)S(1)}, bf16[64,256]{1,0:T(8,128)(2,1)}, u32[]{:S(2)}) copy-start(bf16[64,256]{1,0:T(8,128)(2,1)} %param.15) | copy-start | bytes 98308
  296.6 7.8 %copy-start.5 = (bf16[64,4096]{1,0:T(8,128)(2,1)S(1)}, bf16[64,4096]{1,0:T(8,128)(2,1)}, u32[]{:S(2)}) copy-start(bf16[64,4096]{1,0:T(8,128)(2,1)} %param.14) | copy-start | bytes 1572868
  296.6 8.7 %copy-start.6 = (bf16[1024,256]{1,0:T(8,128)(2,1)S(1)}, bf16[1024,256]{1,0:T(8,128)(2,1)}, u32[]{:S(2)}) copy-start(bf16[1024,256]{1,0:T(8,128)(2,1)} %param.18) | copy-start | bytes 1572868
  296.7 8.7 %copy-start.8 = (bf16[64,256]{1,0:T(8,128)(2,1)S(1)}, bf16[64,256]{1,0:T(8,128)(2,1)}, u32[]{:S(2)}) copy-start(bf16[64,256]{1,0:T(8,128)(2,1)} %param.16) | copy-start | bytes 98308
  296.7 147.0 %all-to-all-start.1 = ((bf16[16,42,4096]{2,1,0:T(8,128)(2,1)}), bf16[16,42,4096]{2,1,0:T(8,128)(2,1)}, u32[]{:S(2)}, u32[]{:S(2)}) async-start(bf16[16,42,4096]{2,1,0:T(8,128)(2,1)} %bitcast.96), calls=%async_computation.2 | async-start | bytes 12582912 | tf_op jit(solution)/shard_map/all_to_all | solution.py:95
  449.9 17.8 %copy-start.1 = (bf16[1,384,4096]{2,1,0:T(8,128)(2,1)S(1)}, bf16[1,384,4096]{2,1,0:T(8,128)(2,1)}, u32[]{:S(2)}) copy-start(bf16[1,384,4096]{2,1,0:T(8,128)(2,1)} %param.24) | copy-start | bytes 9437188
  462.1 3.6 copy-start.2
  462.1 3.6 copy-start.3
Sparse Core Ops, SparseCore 0:
  183.8 23.3 all-gather.2
  273.5 23.1 reduce-scatter.1
where the time goes:
time: 476 us; the launch traced here: 474 us
  waiting for transfers between devices  173 us (36%)
  blocking collectives  144 us (30%)
  local copies, waits for them, and re-layouts  74.5 us (16%)
  matrix products  47.4 us (10%)
  other arithmetic  15.2 us (3%)
  between operations  13.6 us (3%)
  starting transfers between devices  7.33 us (2%)
    all_to_all x1, blocking collectives, local(): lax.all_to_all(send_rows, 'expert', split_axis=0, concat_axis=0, tiled=True)  144 us
    all_to_all x1, waiting for transfers between devices, local(): lax.all_to_all(own_sum.astype(jnp.bfloat16), 'expert', split_axis=0, conc...  126 us
    all_gather x1, waiting for transfers between devices, local(): lax.all_gather(lax.all_to_all(send_rows, 'expert', split_axis=0, concat_a...  23.3 us
    reduce_scatter x1, waiting for transfers between devices, local(): lax.psum_scatter(partial_out.astype(jnp.bfloat16), 'dp', scatter_dimensio...  23.3 us
    dot_general x1, matrix products, expert_rows(): jnp.dot(hidden, down_w, preferred_element_type=jnp.float32)  17.9 us
    all_gather x1, local copies, waits for them, and re-layouts, local(): lax.all_gather(lax.all_to_all(send_rows, 'expert', split_axis=0, concat_a...  14 us
    gather x1, local copies, waits for them, and re-layouts, local(): gathered = results.reshape(owners * capacity, model_width)[places]  12.2 us
    reshape x1, local copies, waits for them, and re-layouts, local(): both_rows.reshape(-1, model_width)  11.9 us
  transfers between devices with their start and end apart: 3, of which 3 were waited for; matrix products, arithmetic and copies ran while one was open for 3% of the time, Pallas kernels for 0%

commit v1 on v0

--- a/solution.py
+++ b/solution.py
@@ -9,6 +9,18 @@
 TOPK = 8
 EXP_DEV = 1
 PREFIX = 1024
+
+
+def sent_to_each(x, axis, split, join):
+    ways, here = (lax.axis_size(axis), lax.axis_index(axis))
+    width = x.shape[split] // ways
+    turned = jnp.roll(x, -here * width, axis=split)
+    got = [lax.slice_in_dim(turned, 0, width, axis=split)]
+    for far in range(1, ways):
+        sent = lax.slice_in_dim(turned, far * width, (far + 1) * width, axis=split)
+        got.append(lax.ppermute(sent, axis, [(d, (d + far) % ways) for d in range(ways)]))
+    line = jnp.concatenate(got[::-1], axis=join)
+    return jnp.roll(line, (here + 1) * got[0].shape[join], axis=join)
 
 
 def attend_rows(queries, keys_local, values_local, prompt_keys, prompt_values):
@@ -82,10 +94,7 @@
         .reshape(owners, capacity, model_width)
     )
     both_rows = lax.all_gather(
-        lax.all_to_all(send_rows, "expert", split_axis=0, concat_axis=0, tiled=True)[None],
-        "dp",
-        axis=0,
-        tiled=True,
+        sent_to_each(send_rows, "expert", 0, 0)[None], "dp", axis=0, tiled=True
     )
     partial_out = expert_rows(both_rows.reshape(-1, model_width), gate_w, up_w, down_w)
     partial_out = partial_out.astype(jnp.float32).reshape(both_rows.shape)

time: 476 us -> 536 us (1.13); the launches traced: 474 us -> 526 us
  blocking collectives: 144 us -> 0 us
  starting transfers between devices: 7.33 us -> 117 us
  waiting for transfers between devices: 173 us -> 237 us
  local copies, waits for them, and re-layouts: 74.5 us -> 85.9 us
  other arithmetic: 15.2 us -> 24.9 us
    all_to_all x1 -> x0, blocking collectives: 144 us -> none  [local(): lax.all_to_all(send_rows, 'expert', split_axis=0, concat_axis=0, tiled=True)]
    ppermute x0 -> x15, starting transfers between devices: none -> 109 us  [sent_to_each(): lax.ppermute(sent, axis, [(d, (d + far) % ways) for d in range(ways)])]
    ppermute x0 -> x15, waiting for transfers between devices: none -> 54.8 us  [sent_to_each(): lax.ppermute(sent, axis, [(d, (d + far) % ways) for d in range(ways)])]
    all_gather x1, waiting for transfers between devices: 23.3 us -> 32.8 us  [local(): lax.all_gather(sent_to_each(send_rows, 'expert', 0, 0)[None], 'dp', axis=...]
    concatenate x0 -> x2, other arithmetic: none -> 8.3 us  [the longest x1 5.15 us: sent_to_each(): turned = jnp.roll(x, -here * width, axis=split)]
    unnamed x22 -> x37, local copies, waits for them, and re-layouts: 1.86 us -> 9.88 us
    dynamic_slice x0 -> x1, local copies, waits for them, and re-layouts: none -> 5.4 us  [sent_to_each(): return jnp.roll(line, (here + 1) * got[0].shape[join], axis=join)]
    all_to_all x1 -> x0, local copies, waits for them, and re-layouts: 5.4 us -> none  [local(): lax.all_to_all(send_rows, 'expert', split_axis=0, concat_axis=0, tiled=True)]
  transfers between devices with their start and end apart: 3 -> 18, of which waited for: 3 -> 9; matrix products, arithmetic and copies ran while one was open for 3% -> 4% of each run, Pallas kernels for 0% -> 0%
where the time goes in v1:
time: 536 us; the launch traced here: 526 us
  waiting for transfers between devices  237 us (44%)
  starting transfers between devices  117 us (22%)
  local copies, waits for them, and re-layouts  85.9 us (16%)
  matrix products  47.3 us (9%)
  other arithmetic  24.9 us (5%)
  between operations  14 us (3%)
    all_to_all x1, waiting for transfers between devices, local(): lax.all_to_all(own_sum.astype(jnp.bfloat16), 'expert', split_axis=0, conc...  126 us
    ppermute x15, starting transfers between devices, sent_to_each(): lax.ppermute(sent, axis, [(d, (d + far) % ways) for d in range(ways)])  109 us
    ppermute x15, waiting for transfers between devices, sent_to_each(): lax.ppermute(sent, axis, [(d, (d + far) % ways) for d in range(ways)])  54.8 us
    all_gather x1, waiting for transfers between devices, local(): lax.all_gather(sent_to_each(send_rows, 'expert', 0, 0)[None], 'dp', axis=...  32.8 us
    reduce_scatter x1, waiting for transfers between devices, local(): lax.psum_scatter(partial_out.astype(jnp.bfloat16), 'dp', scatter_dimensio...  23.3 us
    dot_general x1, matrix products, expert_rows(): jnp.dot(hidden, down_w, preferred_element_type=jnp.float32)  17.9 us
    all_gather x1, local copies, waits for them, and re-layouts, local(): lax.all_gather(sent_to_each(send_rows, 'expert', 0, 0)[None], 'dp', axis=...  14 us
    gather x1, local copies, waits for them, and re-layouts, local(): gathered = results.reshape(owners * capacity, model_width)[places]  12.2 us
  transfers between devices with their start and end apart: 18, of which 9 were waited for; matrix products, arithmetic and copies ran while one was open for 4% of the time, Pallas kernels for 0%

profile of v1, /device:TPU:14, one launch (start us, length us, event | category | flops | bytes accessed | tf_op | source)
XLA Modules:
  0.0 526.2 jit_solution(696704912942831334)
XLA Ops:
  9.7 4.4 compare_select_fusion.2
  15.7 5.6 %fusion.50 = s32[512]{0:T(512)S(1)} fusion(s32[512]{0:T(512)S(1)} %fusion.48, pred[512]{0:T(512)(128)(4,1)S(1)} %get-tuple-element.14, pred[512]{0:T(512)(128)(4,1)S(1)} %get-tuple-element.13, pred[512]{0:T(512)(128)(4,1)S(1)} %get-tuple-element.12, pred[512]{0:T(512)(128)(4,1)S(1)} %get-tuple-element.11, pred[512]{0:T(512)(128)(4,1)S(1)} %get-tuple-element.10, ...), kind=kLoop, calls=%fused_computation.98 | loop fusion | flops 5632 | bytes 10788 | tf_op jit(solution)/shard_map/add | solution.py:85
  23.2 5.2 convolution_convert_fusion.1
  28.4 6.2 %reshape.183 = bf16[16,42,4096]{2,1,0:T(8,128)(2,1)} reshape(bf16[672,4096]{1,0:T(8,128)(2,1)} %convolution_convert_fusion.1) | data formatting | bytes 11010048 | tf_op jit(solution)/shard_map/reshape | solution.py:94
  34.6 5.1 fusion.3
  48.2 3.7 collective-permute-start.3
  51.9 12.9 %collective-permute-done = bf16[1,42,4096]{2,1,0:T(8,128)(2,1)} collective-permute-done((bf16[1,42,4096]{2,1,0:T(8,128)(2,1)}, bf16[1,42,4096]{2,1,0:T(8,128)(2,1)}, u32[]{:S(2)}, u32[]{:S(2)}) %collective-permute-start) | collective-permute-done | bytes 344096 | tf_op jit(solution)/shard_map/ppermute | solution.py:21
  66.8 12.1 %collective-permute-start.6 = (bf16[1,42,4096]{2,1,0:T(8,128)(2,1)}, bf16[1,42,4096]{2,1,0:T(8,128)(2,1)S(1)}, u32[]{:S(2)}, u32[]{:S(2)}) collective-permute-start(bf16[1,42,4096]{2,1,0:T(8,128)(2,1)} %get-tuple-element.25), channel_id=1, source_target_pairs={{0,18},{2,20},{4,22},{6,24},{8,26},{10,28},{12,30},{14,0},{16,2},{... | collective-permute-start | bytes 1032200 | tf_op jit(solution)/shard_map/ppermute | solution.py:21
  81.0 4.3 collective-permute-start.8
  86.4 22.2 %collective-permute-done.4 = bf16[1,42,4096]{2,1,0:T(8,128)(2,1)} collective-permute-done((bf16[1,42,4096]{2,1,0:T(8,128)(2,1)}, bf16[1,42,4096]{2,1,0:T(8,128)(2,1)}, u32[]{:S(2)}, u32[]{:S(2)}) %collective-permute-start.4) | collective-permute-done | bytes 344096 | tf_op jit(solution)/shard_map/ppermute | solution.py:21
  109.6 9.9 %collective-permute-start.10 = (bf16[1,42,4096]{2,1,0:T(8,128)(2,1)}, bf16[1,42,4096]{2,1,0:T(8,128)(2,1)S(1)}, u32[]{:S(2)}, u32[]{:S(2)}) collective-permute-start(bf16[1,42,4096]{2,1,0:T(8,128)(2,1)} %get-tuple-element.21), channel_id=1, source_target_pairs={{0,10},{2,12},{4,14},{6,16},{8,18},{10,20},{12,22},{14,24},{16,26}... | collective-permute-start | bytes 1032200 | tf_op jit(solution)/shard_map/ppermute | solution.py:21
  119.6 3.9 collective-permute-start.11
  127.1 28.2 %collective-permute-start.12 = (bf16[1,42,4096]{2,1,0:T(8,128)(2,1)}, bf16[1,42,4096]{2,1,0:T(8,128)(2,1)S(1)}, u32[]{:S(2)}, u32[]{:S(2)}) collective-permute-start(bf16[1,42,4096]{2,1,0:T(8,128)(2,1)} %get-tuple-element.19), channel_id=1, source_target_pairs={{0,6},{2,8},{4,10},{6,12},{8,14},{10,16},{12,18},{14,20},{16,22},{... | collective-permute-start | bytes 1032200 | tf_op jit(solution)/shard_map/ppermute | solution.py:21
  155.3 33.0 %collective-permute-start.13 = (bf16[1,42,4096]{2,1,0:T(8,128)(2,1)S(1)}, bf16[1,42,4096]{2,1,0:T(8,128)(2,1)S(1)}, u32[]{:S(2)}, u32[]{:S(2)}) collective-permute-start(bf16[1,42,4096]{2,1,0:T(8,128)(2,1)S(1)} %copy-done.6), channel_id=1, source_target_pairs={{0,4},{2,6},{4,8},{6,10},{8,12},{10,14},{12,16},{14,18},{16,20},{1... | collective-permute-start | bytes 1032200 | tf_op jit(solution)/shard_map/ppermute | solution.py:21
  188.4 9.9 %collective-permute-start.14 = (bf16[1,42,4096]{2,1,0:T(8,128)(2,1)S(1)}, bf16[1,42,4096]{2,1,0:T(8,128)(2,1)S(1)}, u32[]{:S(2)}, u32[]{:S(2)}) collective-permute-start(bf16[1,42,4096]{2,1,0:T(8,128)(2,1)S(1)} %get-tuple-element.17), channel_id=1, source_target_pairs={{0,2},{2,4},{4,6},{6,8},{8,10},{10,12},{12,14},{14,16},{16,18},{18... | collective-permute-start | bytes 1032200 | tf_op jit(solution)/shard_map/ppermute | solution.py:21
  198.4 4.0 collective-permute-done.11
  202.5 4.4 collective-permute-done.13
  206.9 7.6 %collective-permute-done.14 = bf16[1,42,4096]{2,1,0:T(8,128)(2,1)S(1)} collective-permute-done((bf16[1,42,4096]{2,1,0:T(8,128)(2,1)S(1)}, bf16[1,42,4096]{2,1,0:T(8,128)(2,1)S(1)}, u32[]{:S(2)}, u32[]{:S(2)}) %collective-permute-start.14) | collective-permute-done | bytes 344096 | tf_op jit(solution)/shard_map/ppermute | solution.py:21
  218.8 5.4 %copy.47 = bf16[16,42,4096]{2,0,1:T(8,128)(2,1)} copy(bf16[16,42,4096]{2,1,0:T(8,128)(2,1)S(1)} %fusion.2) | data formatting | bytes 11010048 | tf_op jit(solution)/shard_map/jit(_roll_dynamic)/dynamic_slice | solution.py:23
  224.7 32.8 %all-gather.3.cloned.1.call-done = bf16[32,42,4096]{2,0,1:T(8,128)(2,1)} async-done(((bf16[16,42,4096]{2,0,1:T(8,128)(2,1)}), bf16[32,42,4096]{2,0,1:T(8,128)(2,1)}) %all-gather.3.cloned.1.call-update) | async-done | bytes 11010064 | tf_op jit(solution)/shard_map/all_gather | solution.py:96
  257.5 14.0 %copy.48 = bf16[32,42,4096]{2,1,0:T(8,128)(2,1)} copy(bf16[32,42,4096]{2,0,1:T(8,128)(2,1)} %all-gather.3.cloned.1.call-done) | data formatting | bytes 22020096 | tf_op jit(solution)/shard_map/all_gather | solution.py:96
  271.6 11.9 %reshape.184 = bf16[1344,4096]{1,0:T(8,128)(2,1)} reshape(bf16[32,42,4096]{2,1,0:T(8,128)(2,1)} %copy.48) | data formatting | bytes 22020096 | tf_op jit(solution)/shard_map/reshape | solution.py:99
  283.4 10.6 %fusion.12 = f32[1344,384]{1,0:T(8,128)} fusion(bf16[1344,4096]{1,0:T(8,128)(2,1)} %reshape.184, bf16[1,4096,384]{2,1,0:T(8,128)(2,1)} %param.24), kind=kOutput, calls=%fused_computation.23 | convolution fusion | flops 4227858432 | bytes 16220160 | tf_op jit(solution)/shard_map/dot_general | solution.py:47
  294.0 17.9 %convolution_convert_fusion = bf16[1344,4096]{1,0:T(8,128)(2,1)} fusion(bf16[1,384,4096]{2,1,0:T(8,128)(2,1)S(1)} %copy-done, bf16[1344,4096]{1,0:T(8,128)(2,1)} %reshape.184, bf16[1,4096,384]{2,1,0:T(8,128)(2,1)} %param.25, f32[1344,384]{1,0:T(8,128)} %fusion.12), kind=kOutput, calls=%fused_computation.2 | convolution fusion | flops 8464318464 | bytes 30375936 | tf_op jit(solution)/shard_map/dot_general | solution.py:50
  311.9 11.7 %convert_element_type.48 = bf16[2,16,42,4096]{3,2,1,0:T(8,128)(2,1)} reshape(bf16[1344,4096]{1,0:T(8,128)(2,1)} %convolution_convert_fusion) | data formatting | bytes 22020096 | tf_op jit(solution)/shard_map/convert_element_type | solution.py:102
  323.6 23.3 %reduce-scatter.2.cloned.1.call-done = bf16[1,16,42,4096]{3,2,1,0:T(8,128)(2,1)} async-done(((bf16[2,16,42,4096]{3,2,1,0:T(8,128)(2,1)}), bf16[1,16,42,4096]{3,2,1,0:T(8,128)(2,1)}) %reduce-scatter.2.cloned.1.call-update) | async-done | bytes 5505040 | tf_op jit(solution)/shard_map/reduce_scatter | solution.py:101
  346.9 7.4 %all-to-all-start = ((bf16[16,42,4096]{2,1,0:T(8,128)(2,1)}), bf16[16,42,4096]{2,1,0:T(8,128)(2,1)}, u32[]{:S(2)}, u32[]{:S(2)}) async-start(bf16[16,42,4096]{2,1,0:T(8,128)(2,1)} %bitcast.96), calls=%async_computation.1 | async-start | bytes 12582912 | tf_op jit(solution)/shard_map/all_to_all | solution.py:104
  356.4 4.3 fusion.60
  360.7 5.9 %fusion.23 = f32[64,2,16,128]{3,0,2,1:T(8,128)S(1)} fusion(bf16[1088,2,128,1]{0,2,3,1:T(8,128)(2,1)S(1)} %bitcast.100, f32[2,16,64]{2,1,0:T(8,128)S(1)} %fusion.60, pred[64,1088]{1,0:T(8,128)(4,1)S(1)} %fusion.41, bf16[1088,2,128,1]{0,2,3,1:T(8,128)(2,1)S(1)} %bitcast.99, bf16[64,2,16,128]{3,2,1,0:T(8,128)(2,1)} %bitcast.103), kind=kOutput, calls=%fused_computation.34 | convolution fusion | flops 1151994880 | bytes 2764800 | tf_op jit(solution)/shard_map/kgts,skd->tkgd/dot_general | solution.py:42
  368.2 125.8 %all-to-all-done = bf16[16,42,4096]{2,1,0:T(8,128)(2,1)} async-done(((bf16[16,42,4096]{2,1,0:T(8,128)(2,1)}), bf16[16,42,4096]{2,1,0:T(8,128)(2,1)}, u32[]{:S(2)}, u32[]{:S(2)}) %all-to-all-start) | async-done | bytes 5505056 | tf_op jit(solution)/shard_map/all_to_all | solution.py:104
  494.0 6.2 %reshape.185 = bf16[672,4096]{1,0:T(8,128)(2,1)} reshape(bf16[16,42,4096]{2,1,0:T(8,128)(2,1)} %all-to-all-done) | data formatting | bytes 11010048 | tf_op jit(solution)/shard_map/reshape | solution.py:107
  500.2 12.2 %gather_fusion = bf16[512,4096]{1,0:T(8,128)(2,1)} fusion(bf16[672,4096]{1,0:T(8,128)(2,1)} %reshape.185, s32[1024]{0:T(1024)S(1)} %pad_clamp_fusion), kind=kCustom, calls=%fused_computation | custom fusion | bytes 8390656 | tf_op jit(solution)/shard_map/gather | solution.py:107
  (93 shorter events, 40.1 us)
Async XLA Ops:
  6.5 287.4 %copy-start = (bf16[1,384,4096]{2,1,0:T(8,128)(2,1)S(1)}, bf16[1,384,4096]{2,1,0:T(8,128)(2,1)}, u32[]{:S(2)}) copy-start(bf16[1,384,4096]{2,1,0:T(8,128)(2,1)} %param.26) | copy-start | bytes 9437188
  6.5 251.0 %all-gather.3.cloned.1.call-start = ((), (), s32[]{:S(2)}) async-start(), calls=%async_computation.3 | async-start | bytes 16515072 | tf_op jit(solution)/shard_map/all_gather | solution.py:96
  39.7 2.7 copy-start.2
  44.8 20.0 %collective-permute-start = (bf16[1,42,4096]{2,1,0:T(8,128)(2,1)}, bf16[1,42,4096]{2,1,0:T(8,128)(2,1)}, u32[]{:S(2)}, u32[]{:S(2)}) collective-permute-start(bf16[1,42,4096]{2,1,0:T(8,128)(2,1)} %get-tuple-element.31), channel_id=1, source_target_pairs={{0,30},{2,0},{4,2},{6,4},{8,6},{10,8},{12,10},{14,12},{16,14},{18,... | collective-permute-start | bytes 1032200 | tf_op jit(solution)/shard_map/ppermute | solution.py:21
  45.3 21.5 %collective-permute-start.1 = (bf16[1,42,4096]{2,1,0:T(8,128)(2,1)}, bf16[1,42,4096]{2,1,0:T(8,128)(2,1)}, u32[]{:S(2)}, u32[]{:S(2)}) collective-permute-start(bf16[1,42,4096]{2,1,0:T(8,128)(2,1)} %get-tuple-element.30), channel_id=1, source_target_pairs={{0,28},{2,30},{4,0},{6,2},{8,4},{10,6},{12,8},{14,10},{16,12},{18,... | collective-permute-start | bytes 1032200 | tf_op jit(solution)/shard_map/ppermute | solution.py:21
  45.8 34.1 %collective-permute-start.2 = (bf16[1,42,4096]{2,1,0:T(8,128)(2,1)}, bf16[1,42,4096]{2,1,0:T(8,128)(2,1)}, u32[]{:S(2)}, u32[]{:S(2)}) collective-permute-start(bf16[1,42,4096]{2,1,0:T(8,128)(2,1)} %get-tuple-element.29), channel_id=1, source_target_pairs={{0,26},{2,28},{4,30},{6,0},{8,2},{10,4},{12,6},{14,8},{16,10},{18,... | collective-permute-start | bytes 1032200 | tf_op jit(solution)/shard_map/ppermute | solution.py:21
  48.2 32.9 %collective-permute-start.3 = (bf16[1,42,4096]{2,1,0:T(8,128)(2,1)}, bf16[1,42,4096]{2,1,0:T(8,128)(2,1)}, u32[]{:S(2)}, u32[]{:S(2)}) collective-permute-start(bf16[1,42,4096]{2,1,0:T(8,128)(2,1)} %get-tuple-element.28), channel_id=1, source_target_pairs={{0,24},{2,26},{4,28},{6,30},{8,0},{10,2},{12,4},{14,6},{16,8},{18,... | collective-permute-start | bytes 1032200 | tf_op jit(solution)/shard_map/ppermute | solution.py:21
  51.8 56.7 %collective-permute-start.4 = (bf16[1,42,4096]{2,1,0:T(8,128)(2,1)}, bf16[1,42,4096]{2,1,0:T(8,128)(2,1)}, u32[]{:S(2)}, u32[]{:S(2)}) collective-permute-start(bf16[1,42,4096]{2,1,0:T(8,128)(2,1)} %get-tuple-element.27), channel_id=1, source_target_pairs={{0,22},{2,24},{4,26},{6,28},{8,30},{10,0},{12,2},{14,4},{16,6},{18... | collective-permute-start | bytes 1032200 | tf_op jit(solution)/shard_map/ppermute | solution.py:21
  51.9 103.5 %copy-start.6 = (bf16[1,42,4096]{2,1,0:T(8,128)(2,1)S(1)}, bf16[1,42,4096]{2,1,0:T(8,128)(2,1)}, u32[]{:S(2)}) copy-start(bf16[1,42,4096]{2,1,0:T(8,128)(2,1)} %get-tuple-element.18) | copy-start | bytes 1032196
  64.8 44.8 %collective-permute-start.5 = (bf16[1,42,4096]{2,1,0:T(8,128)(2,1)}, bf16[1,42,4096]{2,1,0:T(8,128)(2,1)S(1)}, u32[]{:S(2)}, u32[]{:S(2)}) collective-permute-start(bf16[1,42,4096]{2,1,0:T(8,128)(2,1)} %get-tuple-element.26), channel_id=1, source_target_pairs={{0,20},{2,22},{4,24},{6,26},{8,28},{10,30},{12,0},{14,2},{16,4},{1... | collective-permute-start | bytes 1032200 | tf_op jit(solution)/shard_map/ppermute | solution.py:21
  66.8 52.7 %collective-permute-start.6 = (bf16[1,42,4096]{2,1,0:T(8,128)(2,1)}, bf16[1,42,4096]{2,1,0:T(8,128)(2,1)S(1)}, u32[]{:S(2)}, u32[]{:S(2)}) collective-permute-start(bf16[1,42,4096]{2,1,0:T(8,128)(2,1)} %get-tuple-element.25), channel_id=1, source_target_pairs={{0,18},{2,20},{4,22},{6,24},{8,26},{10,28},{12,30},{14,0},{16,2},{... | collective-permute-start | bytes 1032200 | tf_op jit(solution)/shard_map/ppermute | solution.py:21
  79.9 47.1 %collective-permute-start.7 = (bf16[1,42,4096]{2,1,0:T(8,128)(2,1)}, bf16[1,42,4096]{2,1,0:T(8,128)(2,1)S(1)}, u32[]{:S(2)}, u32[]{:S(2)}) collective-permute-start(bf16[1,42,4096]{2,1,0:T(8,128)(2,1)} %get-tuple-element.24), channel_id=1, source_target_pairs={{0,16},{2,18},{4,20},{6,22},{8,24},{10,26},{12,28},{14,30},{16,0},... | collective-permute-start | bytes 1032200 | tf_op jit(solution)/shard_map/ppermute | solution.py:21
  81.0 74.3 %collective-permute-start.8 = (bf16[1,42,4096]{2,1,0:T(8,128)(2,1)}, bf16[1,42,4096]{2,1,0:T(8,128)(2,1)S(1)}, u32[]{:S(2)}, u32[]{:S(2)}) collective-permute-start(bf16[1,42,4096]{2,1,0:T(8,128)(2,1)} %get-tuple-element.23), channel_id=1, source_target_pairs={{0,14},{2,16},{4,18},{6,20},{8,22},{10,24},{12,26},{14,28},{16,30}... | collective-permute-start | bytes 1032200 | tf_op jit(solution)/shard_map/ppermute | solution.py:21
  108.6 79.8 %collective-permute-start.9 = (bf16[1,42,4096]{2,1,0:T(8,128)(2,1)}, bf16[1,42,4096]{2,1,0:T(8,128)(2,1)S(1)}, u32[]{:S(2)}, u32[]{:S(2)}) collective-permute-start(bf16[1,42,4096]{2,1,0:T(8,128)(2,1)} %get-tuple-element.22), channel_id=1, source_target_pairs={{0,12},{2,14},{4,16},{6,18},{8,20},{10,22},{12,24},{14,26},{16,28}... | collective-permute-start | bytes 1032200 | tf_op jit(solution)/shard_map/ppermute | solution.py:21
  109.6 88.7 %collective-permute-start.10 = (bf16[1,42,4096]{2,1,0:T(8,128)(2,1)}, bf16[1,42,4096]{2,1,0:T(8,128)(2,1)S(1)}, u32[]{:S(2)}, u32[]{:S(2)}) collective-permute-start(bf16[1,42,4096]{2,1,0:T(8,128)(2,1)} %get-tuple-element.21), channel_id=1, source_target_pairs={{0,10},{2,12},{4,14},{6,16},{8,18},{10,20},{12,22},{14,24},{16,26}... | collective-permute-start | bytes 1032200 | tf_op jit(solution)/shard_map/ppermute | solution.py:21
  119.6 82.8 %collective-permute-start.11 = (bf16[1,42,4096]{2,1,0:T(8,128)(2,1)}, bf16[1,42,4096]{2,1,0:T(8,128)(2,1)S(1)}, u32[]{:S(2)}, u32[]{:S(2)}) collective-permute-start(bf16[1,42,4096]{2,1,0:T(8,128)(2,1)} %get-tuple-element.20), channel_id=1, source_target_pairs={{0,8},{2,10},{4,12},{6,14},{8,16},{10,18},{12,20},{14,22},{16,24},... | collective-permute-start | bytes 1032200 | tf_op jit(solution)/shard_map/ppermute | solution.py:21
  127.1 75.4 %collective-permute-start.12 = (bf16[1,42,4096]{2,1,0:T(8,128)(2,1)}, bf16[1,42,4096]{2,1,0:T(8,128)(2,1)S(1)}, u32[]{:S(2)}, u32[]{:S(2)}) collective-permute-start(bf16[1,42,4096]{2,1,0:T(8,128)(2,1)} %get-tuple-element.19), channel_id=1, source_target_pairs={{0,6},{2,8},{4,10},{6,12},{8,14},{10,16},{12,18},{14,20},{16,22},{... | collective-permute-start | bytes 1032200 | tf_op jit(solution)/shard_map/ppermute | solution.py:21
  155.3 51.6 %collective-permute-start.13 = (bf16[1,42,4096]{2,1,0:T(8,128)(2,1)S(1)}, bf16[1,42,4096]{2,1,0:T(8,128)(2,1)S(1)}, u32[]{:S(2)}, u32[]{:S(2)}) collective-permute-start(bf16[1,42,4096]{2,1,0:T(8,128)(2,1)S(1)} %copy-done.6), channel_id=1, source_target_pairs={{0,4},{2,6},{4,8},{6,10},{8,12},{10,14},{12,16},{14,18},{16,20},{1... | collective-permute-start | bytes 1032200 | tf_op jit(solution)/shard_map/ppermute | solution.py:21
  188.4 26.2 %collective-permute-start.14 = (bf16[1,42,4096]{2,1,0:T(8,128)(2,1)S(1)}, bf16[1,42,4096]{2,1,0:T(8,128)(2,1)S(1)}, u32[]{:S(2)}, u32[]{:S(2)}) collective-permute-start(bf16[1,42,4096]{2,1,0:T(8,128)(2,1)S(1)} %get-tuple-element.17), channel_id=1, source_target_pairs={{0,2},{2,4},{4,6},{6,8},{8,10},{10,12},{12,14},{14,16},{16,18},{18... | collective-permute-start | bytes 1032200 | tf_op jit(solution)/shard_map/ppermute | solution.py:21
  224.2 122.7 %reduce-scatter.2.cloned.1.call-start = ((), (), s32[]{:S(2)}) async-start(), calls=%async_computation.2 | async-start | bytes 18874368 | tf_op jit(solution)/shard_map/reduce_scatter | solution.py:101
  346.9 7.6 %copy-start.9 = (f32[64,8]{0,1:T(8,128)S(1)}, f32[64,8]{0,1:T(8,128)}, u32[]{:S(2)}) copy-start(f32[64,8]{0,1:T(8,128)} %param.23) | copy-start | bytes 6148
  346.9 7.8 %copy-start.3 = (bf16[1024,256]{1,0:T(8,128)(2,1)S(1)}, bf16[1024,256]{1,0:T(8,128)(2,1)}, u32[]{:S(2)}) copy-start(bf16[1024,256]{1,0:T(8,128)(2,1)} %param.19) | copy-start | bytes 1572868
  346.9 7.8 %copy-start.7 = (bf16[64,256]{1,0:T(8,128)(2,1)S(1)}, bf16[64,256]{1,0:T(8,128)(2,1)}, u32[]{:S(2)}) copy-start(bf16[64,256]{1,0:T(8,128)(2,1)} %param.17) | copy-start | bytes 98308
  346.9 8.2 %copy-start.4 = (bf16[64,4096]{1,0:T(8,128)(2,1)S(1)}, bf16[64,4096]{1,0:T(8,128)(2,1)}, u32[]{:S(2)}) copy-start(bf16[64,4096]{1,0:T(8,128)(2,1)} %param.16) | copy-start | bytes 1572868
  346.9 9.1 %copy-start.5 = (bf16[1024,256]{1,0:T(8,128)(2,1)S(1)}, bf16[1024,256]{1,0:T(8,128)(2,1)}, u32[]{:S(2)}) copy-start(bf16[1024,256]{1,0:T(8,128)(2,1)} %param.20) | copy-start | bytes 1572868
  346.9 9.1 %copy-start.8 = (bf16[64,256]{1,0:T(8,128)(2,1)S(1)}, bf16[64,256]{1,0:T(8,128)(2,1)}, u32[]{:S(2)}) copy-start(bf16[64,256]{1,0:T(8,128)(2,1)} %param.18) | copy-start | bytes 98308
  346.9 147.1 %all-to-all-start = ((bf16[16,42,4096]{2,1,0:T(8,128)(2,1)}), bf16[16,42,4096]{2,1,0:T(8,128)(2,1)}, u32[]{:S(2)}, u32[]{:S(2)}) async-start(bf16[16,42,4096]{2,1,0:T(8,128)(2,1)} %bitcast.96), calls=%async_computation.1 | async-start | bytes 12582912 | tf_op jit(solution)/shard_map/all_to_all | solution.py:104
  500.2 19.0 %copy-start.1 = (bf16[1,384,4096]{2,1,0:T(8,128)(2,1)S(1)}, bf16[1,384,4096]{2,1,0:T(8,128)(2,1)}, u32[]{:S(2)}) copy-start(bf16[1,384,4096]{2,1,0:T(8,128)(2,1)} %param.26) | copy-start | bytes 9437188
Sparse Core Ops, SparseCore 0:
  224.3 33.1 all-gather.2
  323.8 23.1 reduce-scatter.1
